TPU v7x, 512 devices: a whole 4x8x8 slice. The times are simulated.
512 devices in a mesh: chain: 64 (over y, x, core), cols: 8 (over z).
Axes of the slice: x: 4, y: 8, z: 8, core: 2. Of those that a mesh axis runs over, the one named last changes fastest.
Arguments:
- start_vectors: float32 [1024, 256, 256], P('chain', 'cols'), may hold values from -6 to 6
- factors: float32 [1024, 256, 256], P('chain', 'cols'), may hold values from -1.2 to 1.2, as said below
Outputs:
- vectors: float32 [1024, 256, 256], P('chain', 'cols')
- log_growth: float32 [256], P('cols')
Inputs may be any that keep to these rules, and one draw needn't show every extreme that they name: `factors`: the factor blocks of the shifted operator; every product of consecutive factor blocks is bounded.
All inputs are finite; a program needn't handle non-finite values.
Results may differ from a plain program's by a relative error of at most 0.0003.
Values sent between devices are 32-bit elements; how exact they have to be, the bound alone decides.
No kernel may reach another device: no remote copies, remote signals or barrier semaphores. Data moves between devices by JAX's collectives and lax.ppermute only.
A program may use at most 128 MiB of HBM per device.

v0:
```python
import jax
import jax.numpy as jnp
from jax import lax
from jax.sharding import PartitionSpec as P

eps_value = 1e-06


def from_behind(block, axis, distance):
    devices = range(lax.axis_size(axis))
    route = [(i - distance, i) for i in devices if i - distance in devices]
    return lax.ppermute(block, axis, route)


def transform(matrix, vectors_in):
    return lax.dot_general(
        vectors_in,
        matrix,
        (((1,), (1,)), ((), ())),
        precision=lax.Precision.HIGHEST,
        preferred_element_type=jnp.float32,
    )


def compose(later, earlier):
    return jnp.dot(
        later, earlier, precision=lax.Precision.HIGHEST, preferred_element_type=jnp.float32
    )


def forward_rows(factors, right_side, incoming):

    def forward_advance(carried, element):
        matrix, source = element
        carried = transform(matrix, carried) + source
        return (carried, carried)

    return lax.scan(forward_advance, incoming, (factors, right_side))


def backward_rows(factors, forward, incoming):

    def backward_advance(carried, element):
        matrix, source = element
        carried = transform(matrix, source + carried)
        return (carried, carried)

    return lax.scan(backward_advance, incoming, (factors, forward), reverse=True)


def chain_operator(factors, reverse):
    identity_block = jnp.eye(factors.shape[1], dtype=jnp.float32)

    def chain_advance(running, matrix):
        return (compose(matrix, running), None)

    running, _ = lax.scan(chain_advance, identity_block, factors, reverse=reverse)
    return running


def section_count():
    return (lax.axis_size("chain") - 1).bit_length()


def enter_state(summary, direction):
    return from_behind(summary, "chain", direction)


def solve_system(factors, right_side, prefix_forward, prefix_backward):
    zero_state = jnp.zeros(right_side.shape[1:], jnp.float32)
    local_last, _ = forward_rows(factors, right_side, zero_state)
    incoming = enter_state(prefix_forward(local_last), 1)
    _, forward = forward_rows(factors, right_side, incoming)
    local_first, _ = backward_rows(factors, forward, zero_state)
    incoming_back = enter_state(prefix_backward(local_first), -1)
    _, solved = backward_rows(factors, forward, incoming_back)
    return solved


def shards(start_vectors, factors):
    full_factors = lax.all_gather(factors, "cols", axis=1, tiled=True)

    def pair_prefix(operator, summary, direction):
        sections = section_count()
        for section_index in range(sections):
            distance = direction * (1 << section_index)
            if section_index + 1 < sections:
                received_op, received_sum = from_behind((operator, summary), "chain", distance)
                summary = transform(operator, received_sum) + summary
                operator = compose(operator, received_op)
            else:
                received_sum = from_behind(summary, "chain", distance)
                summary = transform(operator, received_sum) + summary
        return summary

    def prefix_forward(summary):
        return pair_prefix(chain_operator(full_factors, False), summary, 1)

    def prefix_backward(summary):
        return pair_prefix(chain_operator(full_factors, True), summary, -1)

    cell_count = start_vectors.shape[0] * lax.axis_size("chain") * start_vectors.shape[2]
    first_solve = solve_system(full_factors, start_vectors, prefix_forward, prefix_backward)
    first_squares = lax.psum(jnp.sum(first_solve * first_solve, axis=(0, 2)), "chain")
    scale_one = jnp.sqrt(first_squares / cell_count + eps_value)
    second_solve = solve_system(
        full_factors, first_solve / scale_one[None, :, None], prefix_forward, prefix_backward
    )
    second_squares = lax.psum(jnp.sum(second_solve * second_solve, axis=(0, 2)), "chain")
    scale_two = jnp.sqrt(second_squares / cell_count + eps_value)
    result_vectors = second_solve / scale_two[None, :, None]
    return (result_vectors, jnp.log(scale_two))


def solution(mesh):
    return jax.shard_map(
        shards,
        mesh=mesh,
        in_specs=(P("chain", "cols", None), P("chain", "cols", None)),
        out_specs=(P("chain", "cols", None), P("cols")),
        check_vma=False,
    )
```

profile of v0, /device:TPU:32, one launch (start us, length us, event | category | flops | bytes accessed | tf_op | source)
XLA Modules:
  0.0 812.4 jit_solution(6026892274242298097)
XLA Ops:
  8.0 64.7 %all-gather.2.cloned.1.call-done = f32[16,256,256]{2,1,0:T(8,128)} async-done(((f32[16,32,256]{2,1,0:T(8,128)}), f32[16,256,256]{2,1,0:T(8,128)}) %all-gather.2.cloned.1.call-update) | async-done | bytes 4194320 | tf_op jit(solution)/shard_map/all_gather | solution.py:81
  72.7 21.4 %while.146 = (s32[]{:T(128)}, f32[32,256]{1,0:T(8,128)S(1)}, f32[16,256,256]{2,1,0:T(8,128)}, f32[16,32,256]{2,1,0:T(8,128)}, s32[]{:T(128)}, /*index=5*/s32[]{:T(128)}) while((s32[]{:T(128)}, f32[32,256]{1,0:T(8,128)S(1)}, f32[16,256,256]{2,1,0:T(8,128)}, f32[16,32,256]{2,1,0:T(8,128)}, s32[]{:T(128)}, /*index=5*/s32[]{:T(128)}) %tuple.241), condition=%wide.region_1.2_spmd.clone, body=%wide.region_0.1_spmd.clone.sunk | while | flops 25182212 | bytes 427087 | solution.py:38
  96.0 22.1 %while.138 = (s32[]{:T(128)}, f32[256,256]{1,0:T(8,128)S(1)}, f32[16,256,256]{2,1,0:T(8,128)}, s32[]{:T(128)}) while((s32[]{:T(128)}, f32[256,256]{1,0:T(8,128)S(1)}, f32[16,256,256]{2,1,0:T(8,128)}, s32[]{:T(128)}) %tuple.273), condition=%wide.region_3.4_spmd, body=%wide.region_2.3_spmd.sunk | while | flops 201326592 | bytes 1311285 | solution.py:57
  134.6 7.3 collective-permute-done.4
  146.4 10.8 %collective-permute-done.6 = f32[256,256]{1,0:T(8,128)S(1)} collective-permute-done((f32[256,256]{1,0:T(8,128)S(1)}, f32[256,256]{1,0:T(8,128)S(1)}, u32[]{:S(2)}, u32[]{:S(2)}) %collective-permute-start.6) | collective-permute-done | bytes 262176 | tf_op jit(solution)/shard_map/ppermute | solution.py:12
  161.9 7.5 collective-permute-done.8
  173.3 7.5 collective-permute-done.10
  190.7 21.4 %while.139 = (s32[]{:T(128)}, f32[32,256]{1,0:T(8,128)S(1)}, f32[16,32,256]{2,1,0:T(8,128)S(1)}, f32[16,256,256]{2,1,0:T(8,128)}, f32[16,32,256]{2,1,0:T(8,128)}, /*index=5*/s32[]{:T(128)}) while((s32[]{:T(128)}, f32[32,256]{1,0:T(8,128)S(1)}, f32[16,32,256]{2,1,0:T(8,128)S(1)}, f32[16,256,256]{2,1,0:T(8,128)}, f32[16,32,256]{2,1,0:T(8,128)}, ...), condition=%wide.region_5.6_spmd, body=%wide.region_4.5_spmd.sunk | while | flops 25174016 | bytes 459845 | solution.py:38
  212.1 21.3 %while.140 = (s32[]{:T(128)}, f32[32,256]{1,0:T(8,128)S(1)}, f32[16,32,256]{2,1,0:T(8,128)S(1)}, f32[16,256,256]{2,1,0:T(8,128)}, s32[]{:T(128)}, /*index=5*/s32[]{:T(128)}) while((s32[]{:T(128)}, f32[32,256]{1,0:T(8,128)S(1)}, f32[16,32,256]{2,1,0:T(8,128)S(1)}, f32[16,256,256]{2,1,0:T(8,128)}, s32[]{:T(128)}, /*index=5*/s32[]{:T(128)}) %tuple.275), condition=%wide.region_7.8_spmd, body=%wide.region_6.7_spmd.sunk | while | flops 25174020 | bytes 427089 | solution.py:48
  235.4 22.1 %while.141 = (s32[]{:T(128)}, f32[256,256]{1,0:T(8,128)S(1)}, f32[16,256,256]{2,1,0:T(8,128)}, s32[]{:T(128)}, s32[]{:T(128)}) while((s32[]{:T(128)}, f32[256,256]{1,0:T(8,128)S(1)}, f32[16,256,256]{2,1,0:T(8,128)}, s32[]{:T(128)}, s32[]{:T(128)}) %tuple.276), condition=%wide.region_9.10_spmd, body=%wide.region_8.9_spmd.sunk | while | flops 201326592 | bytes 1310797 | solution.py:57
  278.5 7.5 collective-permute-done.18
  290.7 6.7 collective-permute-done.20
  301.4 13.4 %collective-permute-done.22 = f32[256,256]{1,0:T(8,128)S(1)} collective-permute-done((f32[256,256]{1,0:T(8,128)S(1)}, f32[256,256]{1,0:T(8,128)S(1)}, u32[]{:S(2)}, u32[]{:S(2)}) %collective-permute-start.22) | collective-permute-done | bytes 262176 | tf_op jit(solution)/shard_map/ppermute | solution.py:12
  322.7 21.6 %while.142 = (s32[]{:T(128)}, f32[32,256]{1,0:T(8,128)S(1)}, f32[16,32,256]{2,1,0:T(8,128)S(1)}, f32[16,32,256]{2,1,0:T(8,128)}, f32[16,256,256]{2,1,0:T(8,128)}, /*index=5*/s32[]{:T(128)}, s32[]{:T(128)}) while((s32[]{:T(128)}, f32[32,256]{1,0:T(8,128)S(1)}, f32[16,32,256]{2,1,0:T(8,128)S(1)}, f32[16,32,256]{2,1,0:T(8,128)}, ...), condition=%wide.region_11.12_spmd, body=%wide.region_10.11_spmd.sunk | while | flops 25174020 | bytes 460377 | solution.py:48
  344.5 129.1 %psum.14 = f32[32]{0:T(128)S(1)} all-reduce(f32[32]{0:T(128)S(1)} %multiply_reduce_fusion.1), channel_id=1, replica_groups=mesh['chain'=64,'cols'=8] {'chain'}, use_global_device_ids=true, to_apply=%region_13.14 | all-reduce | flops 32 | bytes 256 | tf_op jit(solution)/shard_map/psum | solution.py:104
  474.5 21.5 %while.147 = (s32[]{:T(128)}, f32[32,256]{1,0:T(8,128)S(1)}, f32[16,256,256]{2,1,0:T(8,128)}, f32[16,32,256]{2,1,0:T(8,128)}, s32[]{:T(128)}, /*index=5*/s32[]{:T(128)}) while((s32[]{:T(128)}, f32[32,256]{1,0:T(8,128)S(1)}, f32[16,256,256]{2,1,0:T(8,128)}, f32[16,32,256]{2,1,0:T(8,128)}, s32[]{:T(128)}, ...), condition=%wide.region_15.16_spmd.clone, body=%wide.region_14.15_spmd.clone.sunk | while | flops 25182212 | bytes 427087 | solution.py:38
  506.8 7.2 collective-permute-done.25
  516.4 7.5 collective-permute-done.26
  541.4 8.2 %collective-permute-done.29 = f32[32,256]{1,0:T(8,128)S(1)} collective-permute-done((f32[32,256]{1,0:T(8,128)S(1)}, f32[32,256]{1,0:T(8,128)S(1)}, u32[]{:S(2)}, u32[]{:S(2)}) %collective-permute-start.29) | collective-permute-done | bytes 32800 | tf_op jit(solution)/shard_map/ppermute | solution.py:12
  558.6 21.4 %while.143 = (s32[]{:T(128)}, f32[32,256]{1,0:T(8,128)S(1)}, f32[16,32,256]{2,1,0:T(8,128)S(1)}, f32[16,256,256]{2,1,0:T(8,128)}, f32[16,32,256]{2,1,0:T(8,128)}, /*index=5*/s32[]{:T(128)}) while((s32[]{:T(128)}, f32[32,256]{1,0:T(8,128)S(1)}, f32[16,32,256]{2,1,0:T(8,128)S(1)}, f32[16,256,256]{2,1,0:T(8,128)}, f32[16,32,256]{2,1,0:T(8,128)}, ...), condition=%wide.region_17.18_spmd, body=%wide.region_16.17_spmd.sunk | while | flops 25174016 | bytes 459845 | solution.py:38
  580.0 21.3 %while.144 = (s32[]{:T(128)}, f32[32,256]{1,0:T(8,128)S(1)}, f32[16,32,256]{2,1,0:T(8,128)S(1)}, f32[16,256,256]{2,1,0:T(8,128)}, s32[]{:T(128)}, /*index=5*/s32[]{:T(128)}) while((s32[]{:T(128)}, f32[32,256]{1,0:T(8,128)S(1)}, f32[16,32,256]{2,1,0:T(8,128)S(1)}, f32[16,256,256]{2,1,0:T(8,128)}, s32[]{:T(128)}, /*index=5*/s32[]{:T(128)}) %tuple.280), condition=%wide.region_19.20_spmd, body=%wide.region_18.19_spmd.sunk | while | flops 25174020 | bytes 427089 | solution.py:48
  635.6 16.2 %collective-permute-start.37 = (f32[32,256]{1,0:T(8,128)S(1)}, f32[32,256]{1,0:T(8,128)S(1)}, u32[]{:S(2)}, u32[]{:S(2)}) collective-permute-start(f32[32,256]{1,0:T(8,128)S(1)} %convolution_add_fusion), channel_id=1, source_target_pairs={{8,0},{16,8},{24,16},{32,24},{40,32},{48,40},{56,48},{64,56},{72,6... | collective-permute-start | bytes 98312 | tf_op jit(solution)/shard_map/ppermute | solution.py:12
  653.5 21.3 %while.145 = (s32[]{:T(128)}, f32[32,256]{1,0:T(8,128)S(1)}, f32[16,32,256]{2,1,0:T(8,128)S(1)}, f32[16,32,256]{2,1,0:T(8,128)S(1)}, f32[16,256,256]{2,1,0:T(8,128)}, /*index=5*/s32[]{:T(128)}, s32[]{:T(128)}) while((s32[]{:T(128)}, f32[32,256]{1,0:T(8,128)S(1)}, f32[16,32,256]{2,1,0:T(8,128)S(1)}, f32[16,32,256]{2,1,0:T(8,128)S(1)}, ...), condition=%wide.region_21.22_spmd, body=%wide.region_20.21_spmd.sunk | while | flops 25174020 | bytes 460377 | solution.py:48
  675.0 129.1 %psum.15 = f32[32]{0:T(128)S(1)} all-reduce(f32[32]{0:T(128)S(1)} %multiply_reduce_fusion), channel_id=1, replica_groups=mesh['chain'=64,'cols'=8] {'chain'}, use_global_device_ids=true, to_apply=%region_23.24 | all-reduce | flops 32 | bytes 256 | tf_op jit(solution)/shard_map/psum | solution.py:109
  (443 shorter events, 369.9 us)
Async XLA Ops:
  7.2 65.5 %all-gather.2.cloned.1.call-start = ((), (), s32[]{:S(2)}) async-start(), calls=%async_computation | async-start | bytes 4718592 | tf_op jit(solution)/shard_map/all_gather | solution.py:81
  94.1 27.5 %collective-permute-start = (f32[32,256]{1,0:T(8,128)S(1)}, f32[32,256]{1,0:T(8,128)S(1)}, u32[]{:S(2)}, u32[]{:S(2)}) collective-permute-start(f32[32,256]{1,0:T(8,128)S(1)} %get-tuple-element.568), channel_id=1, source_target_pairs={{0,8},{8,16},{16,24},{24,32},{32,40},{40,48},{48,56},{56,64},{64,7... | collective-permute-start | bytes 98312 | tf_op jit(solution)/shard_map/ppermute | solution.py:12
  118.1 11.0 %collective-permute-start.2 = (f32[256,256]{1,0:T(8,128)S(1)}, f32[256,256]{1,0:T(8,128)S(1)}, u32[]{:S(2)}, u32[]{:S(2)}) collective-permute-start(f32[256,256]{1,0:T(8,128)S(1)} %get-tuple-element.569), channel_id=1, source_target_pairs={{0,8},{8,16},{16,24},{24,32},{32,40},{40,48},{48,56},{56,64},{64,7... | collective-permute-start | bytes 786440 | tf_op jit(solution)/shard_map/ppermute | solution.py:12
  122.0 9.5 %collective-permute-start.1 = (f32[32,256]{1,0:T(8,128)S(1)}, f32[32,256]{1,0:T(8,128)S(1)}, u32[]{:S(2)}, u32[]{:S(2)}) collective-permute-start(f32[32,256]{1,0:T(8,128)S(1)} %convolution_add_fusion.23), channel_id=1, source_target_pairs={{0,16},{8,24},{16,32},{24,40},{32,48},{40,56},{48,64},{56,72},{64,... | collective-permute-start | bytes 98312 | tf_op jit(solution)/shard_map/ppermute | solution.py:12
  129.5 12.3 %collective-permute-start.4 = (f32[256,256]{1,0:T(8,128)S(1)}, f32[256,256]{1,0:T(8,128)S(1)}, u32[]{:S(2)}, u32[]{:S(2)}) collective-permute-start(f32[256,256]{1,0:T(8,128)S(1)} %fusion.54), channel_id=1, source_target_pairs={{0,16},{8,24},{16,32},{24,40},{32,48},{40,56},{48,64},{56,72},{64,... | collective-permute-start | bytes 786440 | tf_op jit(solution)/shard_map/ppermute | solution.py:12
  131.8 12.3 %collective-permute-start.3 = (f32[32,256]{1,0:T(8,128)S(1)}, f32[32,256]{1,0:T(8,128)S(1)}, u32[]{:S(2)}, u32[]{:S(2)}) collective-permute-start(f32[32,256]{1,0:T(8,128)S(1)} %convolution_add_fusion.22), channel_id=1, source_target_pairs={{0,32},{8,40},{16,48},{24,56},{32,64},{40,72},{48,80},{56,88},{64,... | collective-permute-start | bytes 98312 | tf_op jit(solution)/shard_map/ppermute | solution.py:12
  142.2 15.0 %collective-permute-start.6 = (f32[256,256]{1,0:T(8,128)S(1)}, f32[256,256]{1,0:T(8,128)S(1)}, u32[]{:S(2)}, u32[]{:S(2)}) collective-permute-start(f32[256,256]{1,0:T(8,128)S(1)} %fusion.55), channel_id=1, source_target_pairs={{0,32},{8,40},{16,48},{24,56},{32,64},{40,72},{48,80},{56,88},{64,... | collective-permute-start | bytes 786440 | tf_op jit(solution)/shard_map/ppermute | solution.py:12
  144.5 15.1 %collective-permute-start.5 = (f32[32,256]{1,0:T(8,128)S(1)}, f32[32,256]{1,0:T(8,128)S(1)}, u32[]{:S(2)}, u32[]{:S(2)}) collective-permute-start(f32[32,256]{1,0:T(8,128)S(1)} %convolution_add_fusion.21), channel_id=1, source_target_pairs={{0,64},{8,72},{16,80},{24,88},{32,96},{40,104},{48,112},{56,120},{... | collective-permute-start | bytes 98312 | tf_op jit(solution)/shard_map/ppermute | solution.py:12
  157.6 11.7 %collective-permute-start.8 = (f32[256,256]{1,0:T(8,128)S(1)}, f32[256,256]{1,0:T(8,128)S(1)}, u32[]{:S(2)}, u32[]{:S(2)}) collective-permute-start(f32[256,256]{1,0:T(8,128)S(1)} %fusion.56), channel_id=1, source_target_pairs={{0,64},{8,72},{16,80},{24,88},{32,96},{40,104},{48,112},{56,120},{... | collective-permute-start | bytes 786440 | tf_op jit(solution)/shard_map/ppermute | solution.py:12
  159.9 11.7 %collective-permute-start.7 = (f32[32,256]{1,0:T(8,128)S(1)}, f32[32,256]{1,0:T(8,128)S(1)}, u32[]{:S(2)}, u32[]{:S(2)}) collective-permute-start(f32[32,256]{1,0:T(8,128)S(1)} %convolution_add_fusion.20), channel_id=1, source_target_pairs={{0,128},{8,136},{16,144},{24,152},{32,160},{40,168},{48,176},{56,1... | collective-permute-start | bytes 98312 | tf_op jit(solution)/shard_map/ppermute | solution.py:12
  169.7 11.1 %collective-permute-start.10 = (f32[256,256]{1,0:T(8,128)S(1)}, f32[256,256]{1,0:T(8,128)S(1)}, u32[]{:S(2)}, u32[]{:S(2)}) collective-permute-start(f32[256,256]{1,0:T(8,128)S(1)} %fusion.57), channel_id=1, source_target_pairs={{0,128},{8,136},{16,144},{24,152},{32,160},{40,168},{48,176},{56,1... | collective-permute-start | bytes 786440 | tf_op jit(solution)/shard_map/ppermute | solution.py:12
  172.0 9.7 %collective-permute-start.9 = (f32[32,256]{1,0:T(8,128)S(1)}, f32[32,256]{1,0:T(8,128)S(1)}, u32[]{:S(2)}, u32[]{:S(2)}) collective-permute-start(f32[32,256]{1,0:T(8,128)S(1)} %convolution_add_fusion.19), channel_id=1, source_target_pairs={{0,256},{8,264},{16,272},{24,280},{32,288},{40,296},{48,304},{56,3... | collective-permute-start | bytes 98312 | tf_op jit(solution)/shard_map/ppermute | solution.py:12
  233.5 26.0 %collective-permute-start.12 = (f32[32,256]{1,0:T(8,128)S(1)}, f32[32,256]{1,0:T(8,128)S(1)}, u32[]{:S(2)}, u32[]{:S(2)}) collective-permute-start(f32[32,256]{1,0:T(8,128)S(1)} %get-tuple-element.571), channel_id=1, source_target_pairs={{8,0},{16,8},{24,16},{32,24},{40,32},{48,40},{56,48},{64,56},{72,6... | collective-permute-start | bytes 98312 | tf_op jit(solution)/shard_map/ppermute | solution.py:12
  264.1 9.8 %collective-permute-start.16 = (f32[256,256]{1,0:T(8,128)S(1)}, f32[256,256]{1,0:T(8,128)S(1)}, u32[]{:S(2)}, u32[]{:S(2)}) collective-permute-start(f32[256,256]{1,0:T(8,128)S(1)} %fusion.59), channel_id=1, source_target_pairs={{16,0},{24,8},{32,16},{40,24},{48,32},{56,40},{64,48},{72,56},{80,... | collective-permute-start | bytes 786440 | tf_op jit(solution)/shard_map/ppermute | solution.py:12
  266.9 9.2 %collective-permute-start.15 = (f32[32,256]{1,0:T(8,128)S(1)}, f32[32,256]{1,0:T(8,128)S(1)}, u32[]{:S(2)}, u32[]{:S(2)}) collective-permute-start(f32[32,256]{1,0:T(8,128)S(1)} %convolution_add_fusion.16), channel_id=1, source_target_pairs={{32,0},{40,8},{48,16},{56,24},{64,32},{72,40},{80,48},{88,56},{96,... | collective-permute-start | bytes 98312 | tf_op jit(solution)/shard_map/ppermute | solution.py:12
  274.3 11.7 %collective-permute-start.18 = (f32[256,256]{1,0:T(8,128)S(1)}, f32[256,256]{1,0:T(8,128)S(1)}, u32[]{:S(2)}, u32[]{:S(2)}) collective-permute-start(f32[256,256]{1,0:T(8,128)S(1)} %fusion.60), channel_id=1, source_target_pairs={{32,0},{40,8},{48,16},{56,24},{64,32},{72,40},{80,48},{88,56},{96,... | collective-permute-start | bytes 786440 | tf_op jit(solution)/shard_map/ppermute | solution.py:12
  276.5 11.9 %collective-permute-start.17 = (f32[32,256]{1,0:T(8,128)S(1)}, f32[32,256]{1,0:T(8,128)S(1)}, u32[]{:S(2)}, u32[]{:S(2)}) collective-permute-start(f32[32,256]{1,0:T(8,128)S(1)} %convolution_add_fusion.15), channel_id=1, source_target_pairs={{64,0},{72,8},{80,16},{88,24},{96,32},{104,40},{112,48},{120,56},{... | collective-permute-start | bytes 98312 | tf_op jit(solution)/shard_map/ppermute | solution.py:12
  286.3 11.1 %collective-permute-start.20 = (f32[256,256]{1,0:T(8,128)S(1)}, f32[256,256]{1,0:T(8,128)S(1)}, u32[]{:S(2)}, u32[]{:S(2)}) collective-permute-start(f32[256,256]{1,0:T(8,128)S(1)} %fusion.61), channel_id=1, source_target_pairs={{64,0},{72,8},{80,16},{88,24},{96,32},{104,40},{112,48},{120,56},{... | collective-permute-start | bytes 786440 | tf_op jit(solution)/shard_map/ppermute | solution.py:12
  288.8 11.0 %collective-permute-start.19 = (f32[32,256]{1,0:T(8,128)S(1)}, f32[32,256]{1,0:T(8,128)S(1)}, u32[]{:S(2)}, u32[]{:S(2)}) collective-permute-start(f32[32,256]{1,0:T(8,128)S(1)} %convolution_add_fusion.14), channel_id=1, source_target_pairs={{128,0},{136,8},{144,16},{152,24},{160,32},{168,40},{176,48},{184,... | collective-permute-start | bytes 98312 | tf_op jit(solution)/shard_map/ppermute | solution.py:12
  297.8 17.0 %collective-permute-start.22 = (f32[256,256]{1,0:T(8,128)S(1)}, f32[256,256]{1,0:T(8,128)S(1)}, u32[]{:S(2)}, u32[]{:S(2)}) collective-permute-start(f32[256,256]{1,0:T(8,128)S(1)} %fusion.62), channel_id=1, source_target_pairs={{128,0},{136,8},{144,16},{152,24},{160,32},{168,40},{176,48},{184,... | collective-permute-start | bytes 786440 | tf_op jit(solution)/shard_map/ppermute | solution.py:12
  300.1 15.1 %collective-permute-start.21 = (f32[32,256]{1,0:T(8,128)S(1)}, f32[32,256]{1,0:T(8,128)S(1)}, u32[]{:S(2)}, u32[]{:S(2)}) collective-permute-start(f32[32,256]{1,0:T(8,128)S(1)} %convolution_add_fusion.13), channel_id=1, source_target_pairs={{256,0},{264,8},{272,16},{280,24},{288,32},{296,40},{304,48},{312,... | collective-permute-start | bytes 98312 | tf_op jit(solution)/shard_map/ppermute | solution.py:12
  514.4 9.6 %collective-permute-start.26 = (f32[32,256]{1,0:T(8,128)S(1)}, f32[32,256]{1,0:T(8,128)S(1)}, u32[]{:S(2)}, u32[]{:S(2)}) collective-permute-start(f32[32,256]{1,0:T(8,128)S(1)} %convolution_add_fusion.10), channel_id=1, source_target_pairs={{0,32},{8,40},{16,48},{24,56},{32,64},{40,72},{48,80},{56,88},{64,... | collective-permute-start | bytes 98312 | tf_op jit(solution)/shard_map/ppermute | solution.py:12
  539.9 9.7 %collective-permute-start.29 = (f32[32,256]{1,0:T(8,128)S(1)}, f32[32,256]{1,0:T(8,128)S(1)}, u32[]{:S(2)}, u32[]{:S(2)}) collective-permute-start(f32[32,256]{1,0:T(8,128)S(1)} %convolution_add_fusion.7), channel_id=1, source_target_pairs={{0,256},{8,264},{16,272},{24,280},{32,288},{40,296},{48,304},{56,3... | collective-permute-start | bytes 98312 | tf_op jit(solution)/shard_map/ppermute | solution.py:12
  635.6 17.8 %collective-permute-start.37 = (f32[32,256]{1,0:T(8,128)S(1)}, f32[32,256]{1,0:T(8,128)S(1)}, u32[]{:S(2)}, u32[]{:S(2)}) collective-permute-start(f32[32,256]{1,0:T(8,128)S(1)} %convolution_add_fusion), channel_id=1, source_target_pairs={{8,0},{16,8},{24,16},{32,24},{40,32},{48,40},{56,48},{64,56},{72,6... | collective-permute-start | bytes 98312 | tf_op jit(solution)/shard_map/ppermute | solution.py:12
  (18 other events, 257.0 us)
Sparse Core Ops, SparseCore 0:
  10.1 62.5 all-gather.1
where the time goes:
time: 818 us; the launch traced here: 812 us
  blocking collectives  258 us (32%)
  matrix products  221 us (27%)
  waiting for transfers between devices  214 us (26%)
  starting transfers between devices  95.2 us (12%)
  between operations  14.9 us (2%)
    dot_general x152, matrix products, transform(): lax.dot_general(vectors_in, matrix, (((1,), (1,)), ((), ())), precision=l...  175 us
    ppermute x38, waiting for transfers between devices, from_behind(): return lax.ppermute(block, axis, route)  148 us
    psum x1, blocking collectives, shards(): lax.psum(jnp.sum(second_solve * second_solve, axis=(0, 2)), 'chain')  129 us
    psum x1, blocking collectives, shards(): lax.psum(jnp.sum(first_solve * first_solve, axis=(0, 2)), 'chain')  129 us
    ppermute x38, starting transfers between devices, from_behind(): return lax.ppermute(block, axis, route)  95.2 us
    all_gather x1, waiting for transfers between devices, shards(): full_factors = lax.all_gather(factors, 'cols', axis=1, tiled=True)  64.7 us
    dot_general x42, matrix products, compose(): jnp.dot(later, earlier, precision=lax.Precision.HIGHEST, preferred_elemen...  46.4 us
  transfers between devices with their start and end apart: 39, of which 29 were waited for; matrix products, arithmetic and copies ran while one was open for 6% of the time, Pallas kernels for 0%

commit v1 on v0

--- a/solution.py
+++ b/solution.py
@@ -106,7 +106,9 @@
     second_solve = solve_system(
         full_factors, first_solve / scale_one[None, :, None], prefix_forward, prefix_backward
     )
-    second_squares = lax.psum(jnp.sum(second_solve * second_solve, axis=(0, 2)), "chain")
+    second_squares = jnp.sum(
+        lax.all_gather(jnp.sum(second_solve * second_solve, axis=(0, 2)), "chain"), axis=0
+    )
     scale_two = jnp.sqrt(second_squares / cell_count + eps_value)
     result_vectors = second_solve / scale_two[None, :, None]
     return (result_vectors, jnp.log(scale_two))

time: 818 us -> 820 us (level)
    unnamed x0 -> x1, blocking collectives: none -> 131 us
    psum x1 -> x0, blocking collectives: 129 us -> none  [shards(): lax.psum(jnp.sum(second_solve * second_solve, axis=(0, 2)), 'chain')]
  transfers between devices with their start and end apart: 39 -> 39, of which waited for: 29 -> 28; matrix products, arithmetic and copies ran while one was open for 6% -> 6% of each run, Pallas kernels for 0% -> 0%
where the time goes in v1:
time: 820 us; the launch traced here: 815 us
  blocking collectives  260 us (32%)
  matrix products  221 us (27%)
  waiting for transfers between devices  212 us (26%)
  starting transfers between devices  95.2 us (12%)
  between operations  15.6 us (2%)
    dot_general x152, matrix products, transform(): lax.dot_general(vectors_in, matrix, (((1,), (1,)), ((), ())), precision=l...  175 us
    ppermute x38, waiting for transfers between devices, from_behind(): return lax.ppermute(block, axis, route)  147 us
    unnamed x1, blocking collectives  131 us
    psum x1, blocking collectives, shards(): lax.psum(jnp.sum(first_solve * first_solve, axis=(0, 2)), 'chain')  129 us
    ppermute x38, starting transfers between devices, from_behind(): return lax.ppermute(block, axis, route)  95.2 us
    all_gather x1, waiting for transfers between devices, shards(): full_factors = lax.all_gather(factors, 'cols', axis=1, tiled=True)  64.7 us
    dot_general x42, matrix products, compose(): jnp.dot(later, earlier, precision=lax.Precision.HIGHEST, preferred_elemen...  46.4 us
  transfers between devices with their start and end apart: 39, of which 28 were waited for; matrix products, arithmetic and copies ran while one was open for 6% of the time, Pallas kernels for 0%

profile of v1, /device:TPU:32, one launch (start us, length us, event | category | flops | bytes accessed | tf_op | source)
XLA Modules:
  0.0 814.8 jit_solution(15860850763824284428)
XLA Ops:
  8.0 64.7 %all-gather.3.cloned.1.call-done = f32[16,256,256]{2,1,0:T(8,128)} async-done(((f32[16,32,256]{2,1,0:T(8,128)}), f32[16,256,256]{2,1,0:T(8,128)}) %all-gather.3.cloned.1.call-update) | async-done | bytes 4194320 | tf_op jit(solution)/shard_map/all_gather | solution.py:81
  72.7 21.5 %while.146 = (s32[]{:T(128)}, f32[32,256]{1,0:T(8,128)S(1)}, f32[16,256,256]{2,1,0:T(8,128)}, f32[16,32,256]{2,1,0:T(8,128)}, s32[]{:T(128)}, /*index=5*/s32[]{:T(128)}) while((s32[]{:T(128)}, f32[32,256]{1,0:T(8,128)S(1)}, f32[16,256,256]{2,1,0:T(8,128)}, f32[16,32,256]{2,1,0:T(8,128)}, s32[]{:T(128)}, /*index=5*/s32[]{:T(128)}) %tuple.241), condition=%wide.region_1.2_spmd.clone, body=%wide.region_0.1_spmd.clone.sunk | while | flops 25182212 | bytes 427087 | solution.py:38
  96.1 22.1 %while.138 = (s32[]{:T(128)}, f32[256,256]{1,0:T(8,128)S(1)}, f32[16,256,256]{2,1,0:T(8,128)}, s32[]{:T(128)}) while((s32[]{:T(128)}, f32[256,256]{1,0:T(8,128)S(1)}, f32[16,256,256]{2,1,0:T(8,128)}, s32[]{:T(128)}) %tuple.273), condition=%wide.region_3.4_spmd, body=%wide.region_2.3_spmd.sunk | while | flops 201326592 | bytes 1311285 | solution.py:57
  134.6 7.3 collective-permute-done.4
  146.5 10.8 %collective-permute-done.6 = f32[256,256]{1,0:T(8,128)S(1)} collective-permute-done((f32[256,256]{1,0:T(8,128)S(1)}, f32[256,256]{1,0:T(8,128)S(1)}, u32[]{:S(2)}, u32[]{:S(2)}) %collective-permute-start.6) | collective-permute-done | bytes 262176 | tf_op jit(solution)/shard_map/ppermute | solution.py:12
  161.9 7.5 collective-permute-done.8
  173.3 7.5 collective-permute-done.10
  190.7 21.4 %while.139 = (s32[]{:T(128)}, f32[32,256]{1,0:T(8,128)S(1)}, f32[16,32,256]{2,1,0:T(8,128)S(1)}, f32[16,256,256]{2,1,0:T(8,128)}, f32[16,32,256]{2,1,0:T(8,128)}, /*index=5*/s32[]{:T(128)}) while((s32[]{:T(128)}, f32[32,256]{1,0:T(8,128)S(1)}, f32[16,32,256]{2,1,0:T(8,128)S(1)}, f32[16,256,256]{2,1,0:T(8,128)}, f32[16,32,256]{2,1,0:T(8,128)}, ...), condition=%wide.region_5.6_spmd, body=%wide.region_4.5_spmd.sunk | while | flops 25174016 | bytes 459845 | solution.py:38
  212.2 21.3 %while.140 = (s32[]{:T(128)}, f32[32,256]{1,0:T(8,128)S(1)}, f32[16,32,256]{2,1,0:T(8,128)S(1)}, f32[16,256,256]{2,1,0:T(8,128)}, s32[]{:T(128)}, /*index=5*/s32[]{:T(128)}) while((s32[]{:T(128)}, f32[32,256]{1,0:T(8,128)S(1)}, f32[16,32,256]{2,1,0:T(8,128)S(1)}, f32[16,256,256]{2,1,0:T(8,128)}, s32[]{:T(128)}, /*index=5*/s32[]{:T(128)}) %tuple.275), condition=%wide.region_7.8_spmd, body=%wide.region_6.7_spmd.sunk | while | flops 25174020 | bytes 427089 | solution.py:48
  235.4 22.1 %while.141 = (s32[]{:T(128)}, f32[256,256]{1,0:T(8,128)S(1)}, f32[16,256,256]{2,1,0:T(8,128)}, s32[]{:T(128)}, s32[]{:T(128)}) while((s32[]{:T(128)}, f32[256,256]{1,0:T(8,128)S(1)}, f32[16,256,256]{2,1,0:T(8,128)}, s32[]{:T(128)}, s32[]{:T(128)}) %tuple.276), condition=%wide.region_9.10_spmd, body=%wide.region_8.9_spmd.sunk | while | flops 201326592 | bytes 1310797 | solution.py:57
  278.5 7.5 collective-permute-done.18
  290.8 6.7 collective-permute-done.20
  301.4 13.4 %collective-permute-done.22 = f32[256,256]{1,0:T(8,128)S(1)} collective-permute-done((f32[256,256]{1,0:T(8,128)S(1)}, f32[256,256]{1,0:T(8,128)S(1)}, u32[]{:S(2)}, u32[]{:S(2)}) %collective-permute-start.22) | collective-permute-done | bytes 262176 | tf_op jit(solution)/shard_map/ppermute | solution.py:12
  322.7 21.6 %while.142 = (s32[]{:T(128)}, f32[32,256]{1,0:T(8,128)S(1)}, f32[16,32,256]{2,1,0:T(8,128)S(1)}, f32[16,32,256]{2,1,0:T(8,128)}, f32[16,256,256]{2,1,0:T(8,128)}, /*index=5*/s32[]{:T(128)}, s32[]{:T(128)}) while((s32[]{:T(128)}, f32[32,256]{1,0:T(8,128)S(1)}, f32[16,32,256]{2,1,0:T(8,128)S(1)}, f32[16,32,256]{2,1,0:T(8,128)}, ...), condition=%wide.region_11.12_spmd, body=%wide.region_10.11_spmd.sunk | while | flops 25174020 | bytes 460377 | solution.py:48
  344.5 129.1 %psum.7 = f32[32]{0:T(128)S(1)} all-reduce(f32[32]{0:T(128)S(1)} %multiply_reduce_fusion.1), channel_id=1, replica_groups=mesh['chain'=64,'cols'=8] {'chain'}, use_global_device_ids=true, to_apply=%region_13.14 | all-reduce | flops 32 | bytes 256 | tf_op jit(solution)/shard_map/psum | solution.py:104
  474.6 21.5 %while.147 = (s32[]{:T(128)}, f32[32,256]{1,0:T(8,128)S(1)}, f32[16,256,256]{2,1,0:T(8,128)}, f32[16,32,256]{2,1,0:T(8,128)}, s32[]{:T(128)}, /*index=5*/s32[]{:T(128)}) while((s32[]{:T(128)}, f32[32,256]{1,0:T(8,128)S(1)}, f32[16,256,256]{2,1,0:T(8,128)}, f32[16,32,256]{2,1,0:T(8,128)}, s32[]{:T(128)}, ...), condition=%wide.region_15.16_spmd.clone, body=%wide.region_14.15_spmd.clone.sunk | while | flops 25182212 | bytes 427087 | solution.py:38
  506.9 7.2 collective-permute-done.25
  516.5 7.5 collective-permute-done.26
  541.4 8.2 %collective-permute-done.29 = f32[32,256]{1,0:T(8,128)S(1)} collective-permute-done((f32[32,256]{1,0:T(8,128)S(1)}, f32[32,256]{1,0:T(8,128)S(1)}, u32[]{:S(2)}, u32[]{:S(2)}) %collective-permute-start.29) | collective-permute-done | bytes 32800 | tf_op jit(solution)/shard_map/ppermute | solution.py:12
  558.6 21.4 %while.143 = (s32[]{:T(128)}, f32[32,256]{1,0:T(8,128)S(1)}, f32[16,32,256]{2,1,0:T(8,128)S(1)}, f32[16,256,256]{2,1,0:T(8,128)}, f32[16,32,256]{2,1,0:T(8,128)}, /*index=5*/s32[]{:T(128)}) while((s32[]{:T(128)}, f32[32,256]{1,0:T(8,128)S(1)}, f32[16,32,256]{2,1,0:T(8,128)S(1)}, f32[16,256,256]{2,1,0:T(8,128)}, f32[16,32,256]{2,1,0:T(8,128)}, ...), condition=%wide.region_17.18_spmd, body=%wide.region_16.17_spmd.sunk | while | flops 25174016 | bytes 459845 | solution.py:38
  580.0 21.3 %while.144 = (s32[]{:T(128)}, f32[32,256]{1,0:T(8,128)S(1)}, f32[16,32,256]{2,1,0:T(8,128)S(1)}, f32[16,256,256]{2,1,0:T(8,128)}, s32[]{:T(128)}, /*index=5*/s32[]{:T(128)}) while((s32[]{:T(128)}, f32[32,256]{1,0:T(8,128)S(1)}, f32[16,32,256]{2,1,0:T(8,128)S(1)}, f32[16,256,256]{2,1,0:T(8,128)}, s32[]{:T(128)}, /*index=5*/s32[]{:T(128)}) %tuple.280), condition=%wide.region_19.20_spmd, body=%wide.region_18.19_spmd.sunk | while | flops 25174020 | bytes 427089 | solution.py:48
  635.7 16.2 %collective-permute-start.37 = (f32[32,256]{1,0:T(8,128)S(1)}, f32[32,256]{1,0:T(8,128)S(1)}, u32[]{:S(2)}, u32[]{:S(2)}) collective-permute-start(f32[32,256]{1,0:T(8,128)S(1)} %convolution_add_fusion), channel_id=1, source_target_pairs={{8,0},{16,8},{24,16},{32,24},{40,32},{48,40},{56,48},{64,56},{72,6... | collective-permute-start | bytes 98312 | tf_op jit(solution)/shard_map/ppermute | solution.py:12
  653.9 21.3 %while.145 = (s32[]{:T(128)}, f32[32,256]{1,0:T(8,128)S(1)}, f32[16,32,256]{2,1,0:T(8,128)S(1)}, f32[16,32,256]{2,1,0:T(8,128)S(1)}, f32[16,256,256]{2,1,0:T(8,128)}, /*index=5*/s32[]{:T(128)}, s32[]{:T(128)}) while((s32[]{:T(128)}, f32[32,256]{1,0:T(8,128)S(1)}, f32[16,32,256]{2,1,0:T(8,128)S(1)}, f32[16,32,256]{2,1,0:T(8,128)S(1)}, ...), condition=%wide.region_21.22_spmd, body=%wide.region_20.21_spmd.sunk | while | flops 25174020 | bytes 460377 | solution.py:48
  675.6 130.8 %all-reduce = f32[2048]{0:T(1024)S(1)} all-reduce(f32[2048]{0:T(1024)S(1)} %dynamic-update-slice), channel_id=2, replica_groups=mesh['chain'=64,'cols'=8] {'chain'}, use_global_device_ids=true, to_apply=%add | all-reduce | flops 2048 | bytes 16384
  (448 shorter events, 369.9 us)
Async XLA Ops:
  7.2 65.5 %all-gather.3.cloned.1.call-start = ((), (), s32[]{:S(2)}) async-start(), calls=%async_computation | async-start | bytes 4718592 | tf_op jit(solution)/shard_map/all_gather | solution.py:81
  94.1 27.5 %collective-permute-start = (f32[32,256]{1,0:T(8,128)S(1)}, f32[32,256]{1,0:T(8,128)S(1)}, u32[]{:S(2)}, u32[]{:S(2)}) collective-permute-start(f32[32,256]{1,0:T(8,128)S(1)} %get-tuple-element.568), channel_id=1, source_target_pairs={{0,8},{8,16},{16,24},{24,32},{32,40},{40,48},{48,56},{56,64},{64,7... | collective-permute-start | bytes 98312 | tf_op jit(solution)/shard_map/ppermute | solution.py:12
  118.2 11.0 %collective-permute-start.2 = (f32[256,256]{1,0:T(8,128)S(1)}, f32[256,256]{1,0:T(8,128)S(1)}, u32[]{:S(2)}, u32[]{:S(2)}) collective-permute-start(f32[256,256]{1,0:T(8,128)S(1)} %get-tuple-element.569), channel_id=1, source_target_pairs={{0,8},{8,16},{16,24},{24,32},{32,40},{40,48},{48,56},{56,64},{64,7... | collective-permute-start | bytes 786440 | tf_op jit(solution)/shard_map/ppermute | solution.py:12
  122.0 9.5 %collective-permute-start.1 = (f32[32,256]{1,0:T(8,128)S(1)}, f32[32,256]{1,0:T(8,128)S(1)}, u32[]{:S(2)}, u32[]{:S(2)}) collective-permute-start(f32[32,256]{1,0:T(8,128)S(1)} %convolution_add_fusion.23), channel_id=1, source_target_pairs={{0,16},{8,24},{16,32},{24,40},{32,48},{40,56},{48,64},{56,72},{64,... | collective-permute-start | bytes 98312 | tf_op jit(solution)/shard_map/ppermute | solution.py:12
  129.6 12.3 %collective-permute-start.4 = (f32[256,256]{1,0:T(8,128)S(1)}, f32[256,256]{1,0:T(8,128)S(1)}, u32[]{:S(2)}, u32[]{:S(2)}) collective-permute-start(f32[256,256]{1,0:T(8,128)S(1)} %fusion.54), channel_id=1, source_target_pairs={{0,16},{8,24},{16,32},{24,40},{32,48},{40,56},{48,64},{56,72},{64,... | collective-permute-start | bytes 786440 | tf_op jit(solution)/shard_map/ppermute | solution.py:12
  131.9 12.3 %collective-permute-start.3 = (f32[32,256]{1,0:T(8,128)S(1)}, f32[32,256]{1,0:T(8,128)S(1)}, u32[]{:S(2)}, u32[]{:S(2)}) collective-permute-start(f32[32,256]{1,0:T(8,128)S(1)} %convolution_add_fusion.22), channel_id=1, source_target_pairs={{0,32},{8,40},{16,48},{24,56},{32,64},{40,72},{48,80},{56,88},{64,... | collective-permute-start | bytes 98312 | tf_op jit(solution)/shard_map/ppermute | solution.py:12
  142.3 15.0 %collective-permute-start.6 = (f32[256,256]{1,0:T(8,128)S(1)}, f32[256,256]{1,0:T(8,128)S(1)}, u32[]{:S(2)}, u32[]{:S(2)}) collective-permute-start(f32[256,256]{1,0:T(8,128)S(1)} %fusion.55), channel_id=1, source_target_pairs={{0,32},{8,40},{16,48},{24,56},{32,64},{40,72},{48,80},{56,88},{64,... | collective-permute-start | bytes 786440 | tf_op jit(solution)/shard_map/ppermute | solution.py:12
  144.5 15.1 %collective-permute-start.5 = (f32[32,256]{1,0:T(8,128)S(1)}, f32[32,256]{1,0:T(8,128)S(1)}, u32[]{:S(2)}, u32[]{:S(2)}) collective-permute-start(f32[32,256]{1,0:T(8,128)S(1)} %convolution_add_fusion.21), channel_id=1, source_target_pairs={{0,64},{8,72},{16,80},{24,88},{32,96},{40,104},{48,112},{56,120},{... | collective-permute-start | bytes 98312 | tf_op jit(solution)/shard_map/ppermute | solution.py:12
  157.7 11.7 %collective-permute-start.8 = (f32[256,256]{1,0:T(8,128)S(1)}, f32[256,256]{1,0:T(8,128)S(1)}, u32[]{:S(2)}, u32[]{:S(2)}) collective-permute-start(f32[256,256]{1,0:T(8,128)S(1)} %fusion.56), channel_id=1, source_target_pairs={{0,64},{8,72},{16,80},{24,88},{32,96},{40,104},{48,112},{56,120},{... | collective-permute-start | bytes 786440 | tf_op jit(solution)/shard_map/ppermute | solution.py:12
  160.0 11.7 %collective-permute-start.7 = (f32[32,256]{1,0:T(8,128)S(1)}, f32[32,256]{1,0:T(8,128)S(1)}, u32[]{:S(2)}, u32[]{:S(2)}) collective-permute-start(f32[32,256]{1,0:T(8,128)S(1)} %convolution_add_fusion.20), channel_id=1, source_target_pairs={{0,128},{8,136},{16,144},{24,152},{32,160},{40,168},{48,176},{56,1... | collective-permute-start | bytes 98312 | tf_op jit(solution)/shard_map/ppermute | solution.py:12
  169.8 11.1 %collective-permute-start.10 = (f32[256,256]{1,0:T(8,128)S(1)}, f32[256,256]{1,0:T(8,128)S(1)}, u32[]{:S(2)}, u32[]{:S(2)}) collective-permute-start(f32[256,256]{1,0:T(8,128)S(1)} %fusion.57), channel_id=1, source_target_pairs={{0,128},{8,136},{16,144},{24,152},{32,160},{40,168},{48,176},{56,1... | collective-permute-start | bytes 786440 | tf_op jit(solution)/shard_map/ppermute | solution.py:12
  172.0 9.7 %collective-permute-start.9 = (f32[32,256]{1,0:T(8,128)S(1)}, f32[32,256]{1,0:T(8,128)S(1)}, u32[]{:S(2)}, u32[]{:S(2)}) collective-permute-start(f32[32,256]{1,0:T(8,128)S(1)} %convolution_add_fusion.19), channel_id=1, source_target_pairs={{0,256},{8,264},{16,272},{24,280},{32,288},{40,296},{48,304},{56,3... | collective-permute-start | bytes 98312 | tf_op jit(solution)/shard_map/ppermute | solution.py:12
  233.5 26.0 %collective-permute-start.12 = (f32[32,256]{1,0:T(8,128)S(1)}, f32[32,256]{1,0:T(8,128)S(1)}, u32[]{:S(2)}, u32[]{:S(2)}) collective-permute-start(f32[32,256]{1,0:T(8,128)S(1)} %get-tuple-element.571), channel_id=1, source_target_pairs={{8,0},{16,8},{24,16},{32,24},{40,32},{48,40},{56,48},{64,56},{72,6... | collective-permute-start | bytes 98312 | tf_op jit(solution)/shard_map/ppermute | solution.py:12
  264.1 9.8 %collective-permute-start.16 = (f32[256,256]{1,0:T(8,128)S(1)}, f32[256,256]{1,0:T(8,128)S(1)}, u32[]{:S(2)}, u32[]{:S(2)}) collective-permute-start(f32[256,256]{1,0:T(8,128)S(1)} %fusion.59), channel_id=1, source_target_pairs={{16,0},{24,8},{32,16},{40,24},{48,32},{56,40},{64,48},{72,56},{80,... | collective-permute-start | bytes 786440 | tf_op jit(solution)/shard_map/ppermute | solution.py:12
  267.0 9.2 %collective-permute-start.15 = (f32[32,256]{1,0:T(8,128)S(1)}, f32[32,256]{1,0:T(8,128)S(1)}, u32[]{:S(2)}, u32[]{:S(2)}) collective-permute-start(f32[32,256]{1,0:T(8,128)S(1)} %convolution_add_fusion.16), channel_id=1, source_target_pairs={{32,0},{40,8},{48,16},{56,24},{64,32},{72,40},{80,48},{88,56},{96,... | collective-permute-start | bytes 98312 | tf_op jit(solution)/shard_map/ppermute | solution.py:12
  274.3 11.7 %collective-permute-start.18 = (f32[256,256]{1,0:T(8,128)S(1)}, f32[256,256]{1,0:T(8,128)S(1)}, u32[]{:S(2)}, u32[]{:S(2)}) collective-permute-start(f32[256,256]{1,0:T(8,128)S(1)} %fusion.60), channel_id=1, source_target_pairs={{32,0},{40,8},{48,16},{56,24},{64,32},{72,40},{80,48},{88,56},{96,... | collective-permute-start | bytes 786440 | tf_op jit(solution)/shard_map/ppermute | solution.py:12
  276.6 11.9 %collective-permute-start.17 = (f32[32,256]{1,0:T(8,128)S(1)}, f32[32,256]{1,0:T(8,128)S(1)}, u32[]{:S(2)}, u32[]{:S(2)}) collective-permute-start(f32[32,256]{1,0:T(8,128)S(1)} %convolution_add_fusion.15), channel_id=1, source_target_pairs={{64,0},{72,8},{80,16},{88,24},{96,32},{104,40},{112,48},{120,56},{... | collective-permute-start | bytes 98312 | tf_op jit(solution)/shard_map/ppermute | solution.py:12
  286.3 11.1 %collective-permute-start.20 = (f32[256,256]{1,0:T(8,128)S(1)}, f32[256,256]{1,0:T(8,128)S(1)}, u32[]{:S(2)}, u32[]{:S(2)}) collective-permute-start(f32[256,256]{1,0:T(8,128)S(1)} %fusion.61), channel_id=1, source_target_pairs={{64,0},{72,8},{80,16},{88,24},{96,32},{104,40},{112,48},{120,56},{... | collective-permute-start | bytes 786440 | tf_op jit(solution)/shard_map/ppermute | solution.py:12
  288.8 11.0 %collective-permute-start.19 = (f32[32,256]{1,0:T(8,128)S(1)}, f32[32,256]{1,0:T(8,128)S(1)}, u32[]{:S(2)}, u32[]{:S(2)}) collective-permute-start(f32[32,256]{1,0:T(8,128)S(1)} %convolution_add_fusion.14), channel_id=1, source_target_pairs={{128,0},{136,8},{144,16},{152,24},{160,32},{168,40},{176,48},{184,... | collective-permute-start | bytes 98312 | tf_op jit(solution)/shard_map/ppermute | solution.py:12
  297.8 17.0 %collective-permute-start.22 = (f32[256,256]{1,0:T(8,128)S(1)}, f32[256,256]{1,0:T(8,128)S(1)}, u32[]{:S(2)}, u32[]{:S(2)}) collective-permute-start(f32[256,256]{1,0:T(8,128)S(1)} %fusion.62), channel_id=1, source_target_pairs={{128,0},{136,8},{144,16},{152,24},{160,32},{168,40},{176,48},{184,... | collective-permute-start | bytes 786440 | tf_op jit(solution)/shard_map/ppermute | solution.py:12
  300.1 15.1 %collective-permute-start.21 = (f32[32,256]{1,0:T(8,128)S(1)}, f32[32,256]{1,0:T(8,128)S(1)}, u32[]{:S(2)}, u32[]{:S(2)}) collective-permute-start(f32[32,256]{1,0:T(8,128)S(1)} %convolution_add_fusion.13), channel_id=1, source_target_pairs={{256,0},{264,8},{272,16},{280,24},{288,32},{296,40},{304,48},{312,... | collective-permute-start | bytes 98312 | tf_op jit(solution)/shard_map/ppermute | solution.py:12
  514.4 9.6 %collective-permute-start.26 = (f32[32,256]{1,0:T(8,128)S(1)}, f32[32,256]{1,0:T(8,128)S(1)}, u32[]{:S(2)}, u32[]{:S(2)}) collective-permute-start(f32[32,256]{1,0:T(8,128)S(1)} %convolution_add_fusion.10), channel_id=1, source_target_pairs={{0,32},{8,40},{16,48},{24,56},{32,64},{40,72},{48,80},{56,88},{64,... | collective-permute-start | bytes 98312 | tf_op jit(solution)/shard_map/ppermute | solution.py:12
  539.9 9.7 %collective-permute-start.29 = (f32[32,256]{1,0:T(8,128)S(1)}, f32[32,256]{1,0:T(8,128)S(1)}, u32[]{:S(2)}, u32[]{:S(2)}) collective-permute-start(f32[32,256]{1,0:T(8,128)S(1)} %convolution_add_fusion.7), channel_id=1, source_target_pairs={{0,256},{8,264},{16,272},{24,280},{32,288},{40,296},{48,304},{56,3... | collective-permute-start | bytes 98312 | tf_op jit(solution)/shard_map/ppermute | solution.py:12
  635.7 18.2 %collective-permute-start.37 = (f32[32,256]{1,0:T(8,128)S(1)}, f32[32,256]{1,0:T(8,128)S(1)}, u32[]{:S(2)}, u32[]{:S(2)}) collective-permute-start(f32[32,256]{1,0:T(8,128)S(1)} %convolution_add_fusion), channel_id=1, source_target_pairs={{8,0},{16,8},{24,16},{32,24},{40,32},{48,40},{56,48},{64,56},{72,6... | collective-permute-start | bytes 98312 | tf_op jit(solution)/shard_map/ppermute | solution.py:12
  (18 other events, 257.0 us)
Sparse Core Ops, SparseCore 0:
  10.1 62.5 all-gather.2
